TPU v7x, 32 devices: a whole 2x2x4 slice. The times are simulated.
32 devices in a mesh: lat: 8 (over y, x, core), lon: 4 (over z).
Axes of the slice: x: 2, y: 2, z: 4, core: 2. Of those that a mesh axis runs over, the one named last changes fastest.
Arguments:
- adjoint: float32 [8, 8, 256, 512], P(None, None, 'lat', 'lon'), may hold values from -6 to 6
- transport: float32 [6, 8, 256, 512], P(None, None, 'lat', 'lon'), may hold values from 0.03 to 0.14
- cell_weight: float32 [256, 512], P('lat', 'lon'), may hold values from 0.1 to 1
- region_local: int32 [256, 512], P('lat', 'lon'), may hold values from 0 to 255
- tile_regions: int32 [32, 256], replicated, may hold values from 0 to 2047, as said below
- polar_rows: int32 [256], P('lat'), may hold values 0 or 1
- week_index: int32 [1], replicated, may hold values from 0 to 51
- grad_in: bfloat16 [2048, 416], P(('lat', 'lon')), may hold values from -6 to 6
- covariance: bfloat16 [2048, 2048], P(('lat', 'lon')), may hold values from -0.25 to 0.25
Outputs:
- adjoint_out: float32 [8, 8, 256, 512], P(None, None, 'lat', 'lon')
- precond: float32 [2048, 416], P(('lat', 'lon'))
Inputs may be any that keep to these rules, and one draw needn't show every extreme that they name: `tile_regions`: each row holds 256 different region numbers; with per = 8, entries o * per to o * per + per - 1 of a row lie in regions o * 64 to o * 64 + 63, for every o.
All inputs are finite; a program needn't handle non-finite values. No bound on the sum of `polar_rows` on one device may be relied on, other than what follows from the above.
Results may differ from a plain program's by a relative error of at most 0.00066.
Values may be sent and summed in bfloat16 or wider, within the bound.
No kernel may reach another device: no remote copies, remote signals or barrier semaphores. Data moves between devices by JAX's collectives and lax.ppermute only.
A program may use at most 128 MiB of HBM per device.

v0:
```python
import jax
import jax.numpy as jnp
from jax import lax
from jax.sharding import PartitionSpec as P


def extended(x, sides, width):
    for axis, dim in sides:
        size, length = (lax.axis_size(axis), x.shape[dim])
        up = [(i, (i + 1) % size) for i in range(size)]
        down = [(j, i) for i, j in up]
        last = lax.slice_in_dim(x, length - width, length, axis=dim)
        leading = lax.slice_in_dim(x, 0, width, axis=dim)
        before = lax.ppermute(last, axis, up)
        after = lax.ppermute(leading, axis, down)
        x = jnp.concatenate([before, x, after], axis=dim)
    return x


def advance(padded, rates):
    centre = padded[:, :, 1:-1, 1:-1]
    to_east = padded[:, :, 1:-1, 2:] - centre
    to_west = padded[:, :, 1:-1, :-2] - centre
    to_north = padded[:, :, 2:, 1:-1] - centre
    to_south = padded[:, :, :-2, 1:-1] - centre
    flat_zero = jnp.zeros_like(centre[:, :1])
    upper = jnp.concatenate([centre[:, 1:] - centre[:, :-1], flat_zero], axis=1)
    lower = jnp.concatenate([flat_zero, centre[:, :-1] - centre[:, 1:]], axis=1)
    return (
        centre
        + rates[0] * to_east
        + rates[1] * to_west
        + rates[2] * to_north
        + rates[3] * to_south
        + rates[4] * upper
        + rates[5] * lower
    )


def pole_mask(padded, margin, interior):
    band = lax.axis_index("lat")
    last_band = lax.axis_size("lat") - 1
    row_ids = jnp.arange(interior + 2 * margin, dtype=jnp.int32)
    outside = (row_ids < margin) & (band == 0) | (row_ids >= interior + margin) & (
        band == last_band
    )
    return jnp.where(outside[None, None, :, None], 0.0, padded)


def shards(
    adjoint,
    transport,
    cell_weight,
    region_local,
    tile_regions,
    polar_rows,
    week_index,
    grad_in,
    covariance,
):
    tracers, levels, lat_rows, lon_cols = adjoint.shape
    region_count = covariance.shape[1]
    own_rows = covariance.shape[0]
    week_cols = grad_in.shape[1] // tracers
    lon_count = lax.axis_size("lon")
    my_tile = lax.axis_index("lat") * lon_count + lax.axis_index("lon")
    base = jnp.dot(
        covariance,
        lax.all_gather(grad_in, ("lat", "lon"), axis=0, tiled=True),
        preferred_element_type=jnp.float32,
    )
    field = adjoint
    for repeat in range(2):
        padded = extended(field, (("lat", 2), ("lon", 3)), 1)
        field = advance(pole_mask(padded, 1, lat_rows), transport)
    row_sums = lax.psum(jnp.sum(field, axis=3), "lon")
    zonal = row_sums / (lon_cols * lon_count)
    flags = polar_rows.astype(jnp.float32)[None, None, :, None]
    adjoint_out = field + 0.5 * flags * (zonal[..., None] - field)
    surface = (adjoint_out[:, 0] * cell_weight[None]).reshape(tracers, -1)
    local_count = tile_regions.shape[1]
    one_hot = (
        region_local.reshape(1, -1) == jnp.arange(local_count, dtype=jnp.int32)[:, None]
    ).astype(jnp.float32)
    local_sums = lax.dot_general(
        one_hot,
        surface,
        (((1,), (1,)), ((), ())),
        precision=lax.Precision.HIGHEST,
        preferred_element_type=jnp.float32,
    )
    my_regions = lax.dynamic_index_in_dim(tile_regions, my_tile, 0, keepdims=False)
    dense = jnp.zeros((region_count, tracers), jnp.float32).at[my_regions].add(local_sums)
    fresh_all = lax.psum(dense, ("lat", "lon")).astype(jnp.bfloat16)
    added = jnp.dot(covariance, fresh_all, preferred_element_type=jnp.float32)
    week_hot = (jnp.arange(week_cols, dtype=jnp.int32) == week_index[0]).astype(jnp.float32)
    precond = (
        base.reshape(own_rows, week_cols, tracers) + week_hot[None, :, None] * added[:, None, :]
    )
    return (adjoint_out, precond.reshape(own_rows, week_cols * tracers))


def solution(mesh):
    in_specs = (
        P(None, None, "lat", "lon"),
        P(None, None, "lat", "lon"),
        P("lat", "lon"),
        P("lat", "lon"),
        P(),
        P("lat"),
        P(),
        P(("lat", "lon"), None),
        P(("lat", "lon"), None),
    )
    out_specs = (P(None, None, "lat", "lon"), P(("lat", "lon"), None))
    return jax.shard_map(shards, mesh=mesh, in_specs=in_specs, out_specs=out_specs, check_vma=False)
```

profile of v0, /device:TPU:0, one launch (start us, length us, event | category | flops | bytes accessed | tf_op | source)
XLA Modules:
  0.0 179.2 jit_solution(4061105329152444854)
XLA Ops:
  7.2 0.0 copy-start
  7.2 0.0 all-gather.2.cloned.1.call-start
  7.2 1.1 fusion.30
  8.3 0.5 collective-permute-start
  8.9 2.9 %collective-permute-start.1 = (f32[8,8,1,128]{3,1,2,0:T(8,128)S(1)}, f32[8,8,1,128]{3,1,2,0:T(8,128)S(1)}, u32[]{:S(2)}, u32[]{:S(2)}) collective-permute-start(f32[8,8,1,128]{3,1,2,0:T(8,128)S(1)} %bitcast.36), channel_id=1, source_target_pairs={{4,0},{8,4},{12,8},{16,12},{20,16},{24,20},{28,24},{0,28},{5,1},{9... | collective-permute-start | bytes 98312 | tf_op jit(solution)/shard_map/ppermute | solution.py:15
  11.8 0.0 all-gather.2.cloned.1.call-update
  11.8 1.3 slice_bitcast_fusion.5
  13.1 0.7 convert_multiply_fusion
  13.8 3.6 %copy.81 = f32[8,8,32,128]{2,1,3,0:T(8,128)} copy(f32[8,8,32,128]{3,2,1,0:T(8,128)} %param.9) | data formatting | bytes 2097152 | tf_op args[0]
  17.4 0.0 collective-permute-done
  17.4 2.6 %copy.80 = f32[8,8,1,128]{2,1,3,0:T(8,128)} copy(f32[8,8,1,128]{3,1,2,0:T(8,128)S(1)} %collective-permute-done) | data formatting | bytes 65536 | tf_op jit(solution)/shard_map/ppermute | solution.py:14
  20.1 0.0 collective-permute-done.1
  20.1 2.6 %copy.82 = f32[8,8,1,128]{2,1,3,0:T(8,128)} copy(f32[8,8,1,128]{3,1,2,0:T(8,128)S(1)} %collective-permute-done.1) | data formatting | bytes 65536 | tf_op jit(solution)/shard_map/ppermute | solution.py:15
  22.7 0.9 pad_maximum_fusion.5
  23.6 2.3 %collective-permute-start.2 = (f32[8,8,34,1]{2,1,3,0:T(8,128)S(1)}, f32[8,8,34,1]{2,1,3,0:T(8,128)S(1)}, u32[]{:S(2)}, u32[]{:S(2)}) collective-permute-start(f32[8,8,34,1]{2,1,3,0:T(8,128)S(1)} %get-tuple-element.16), channel_id=1, source_target_pairs={{0,1},{1,2},{2,3},{3,0},{4,5},{5,6},{6,7},{7,4},{8,9},{9,10},{10,1... | collective-permute-start | bytes 26120 | tf_op jit(solution)/shard_map/ppermute | solution.py:14
  26.0 2.1 %collective-permute-start.3 = (f32[8,8,34,1]{2,1,3,0:T(8,128)S(1)}, f32[8,8,34,1]{2,1,3,0:T(8,128)S(1)}, u32[]{:S(2)}, u32[]{:S(2)}) collective-permute-start(f32[8,8,34,1]{2,1,3,0:T(8,128)S(1)} %get-tuple-element.17), channel_id=1, source_target_pairs={{1,0},{2,1},{3,2},{0,3},{5,4},{6,5},{7,6},{4,7},{9,8},{10,9},{11,1... | collective-permute-start | bytes 26120 | tf_op jit(solution)/shard_map/ppermute | solution.py:15
  28.1 0.2 copy.83
  28.3 1.0 copy.84
  29.3 1.0 copy.85
  30.3 1.0 copy.86
  31.4 1.0 copy.87
  32.4 1.0 copy.88
  33.4 0.0 collective-permute-done.2
  33.4 0.0 collective-permute-done.3
  33.4 5.8 %maximum_select_fusion = f32[8,8,34,130]{2,1,3,0:T(8,128)S(1)} fusion(f32[8,8,34,1]{2,1,3,0:T(8,128)S(1)} %collective-permute-done.3, f32[8,8,1,128]{2,1,3,0:T(8,128)} %copy.82, f32[8,8,32,128]{2,1,3,0:T(8,128)} %copy.81, f32[8,8,1,128]{2,1,3,0:T(8,128)} %copy.80, f32[8,8,34,1]{2,1,3,0:T(8,128)S(1)} %collective-permute-done.2, pred[34]{0:T(512)(128)(4,1)S(1)} %and_or_fusion), kind=kLoop, calls=%fused_computation.1 | loop fusion | flops 1414400 | bytes 2263074 | tf_op jit(solution)/shard_map/jit(_where)/select_n | solution.py:47
  39.2 2.2 %slice_subtract_fusion.11 = (f32[8,7,32,128]{2,1,3,0:T(8,128)S(1)}, f32[8,7,32,128]{2,1,3,0:T(8,128)S(1)}) fusion(f32[8,8,34,130]{2,1,3,0:T(8,128)S(1)} %maximum_select_fusion), kind=kLoop, calls=%fused_computation.37 | loop fusion | flops 458752 | bytes 3670016 | tf_op jit(solution)/shard_map/sub | solution.py:27
  41.4 6.1 %fusion.13 = f32[8,8,32,128]{2,1,3,0:T(8,128)S(1)} fusion(f32[8,8,34,130]{2,1,3,0:T(8,128)S(1)} %maximum_select_fusion, f32[8,7,32,128]{2,1,3,0:T(8,128)S(1)} %get-tuple-element.21, f32[8,7,32,128]{2,1,3,0:T(8,128)S(1)} %get-tuple-element.20, f32[8,32,128]{1,0,2:T(8,128)} %copy.88, f32[8,32,128]{1,0,2:T(8,128)} %copy.87, f32[8,32,128]{1,0,2:T(8,128)} %copy.86, ...), kind=kLoop, calls=%fused_computation.21 | loop fusion | flops 4194304 | bytes 8912896 | tf_op jit(solution)/shard_map/add | solution.py:30
  47.6 0.0 copy-start.1
  47.6 4.6 %fusion.29 = (f32[8,8,1,128]{2,1,3,0:T(8,128)}, f32[8,8,1,128]{2,1,3,0:T(8,128)}) fusion(f32[8,8,32,128]{2,1,3,0:T(8,128)S(1)} %fusion.13), kind=kLoop, calls=%fused_computation.66 | loop fusion | bytes 131072 | tf_op jit(solution)/shard_map/slice | solution.py:12
  52.2 0.0 copy-done.1
  52.2 2.8 %copy.89 = f32[8,8,1,128]{3,1,2,0:T(8,128)S(1)} copy(f32[8,8,1,128]{2,1,3,0:T(8,128)} %get-tuple-element.22) | data formatting | bytes 65536 | tf_op jit(solution)/shard_map/slice | solution.py:12
  55.1 0.0 collective-permute-start.4
  55.1 2.9 %copy.90 = f32[8,8,1,128]{3,1,2,0:T(8,128)S(1)} copy(f32[8,8,1,128]{2,1,3,0:T(8,128)} %get-tuple-element.23) | data formatting | bytes 65536 | tf_op jit(solution)/shard_map/slice | solution.py:13
  58.0 2.9 %collective-permute-start.5 = (f32[8,8,1,128]{3,1,2,0:T(8,128)S(1)}, f32[8,8,1,128]{3,1,2,0:T(8,128)S(1)}, u32[]{:S(2)}, u32[]{:S(2)}) collective-permute-start(f32[8,8,1,128]{3,1,2,0:T(8,128)S(1)} %copy.90), channel_id=1, source_target_pairs={{4,0},{8,4},{12,8},{16,12},{20,16},{24,20},{28,24},{0,28},{5,1},{9... | collective-permute-start | bytes 98312 | tf_op jit(solution)/shard_map/ppermute | solution.py:15
  60.8 0.7 compare_select_fusion
  62.2 0.0 collective-permute-done.4
  62.2 2.7 %copy.91 = f32[8,8,1,128]{2,1,3,0:T(8,128)} copy(f32[8,8,1,128]{3,1,2,0:T(8,128)S(1)} %collective-permute-done.4) | data formatting | bytes 65536 | tf_op jit(solution)/shard_map/ppermute | solution.py:14
  64.9 0.0 collective-permute-done.5
  64.9 2.7 %copy.92 = f32[8,8,1,128]{2,1,3,0:T(8,128)} copy(f32[8,8,1,128]{3,1,2,0:T(8,128)S(1)} %collective-permute-done.5) | data formatting | bytes 65536 | tf_op jit(solution)/shard_map/ppermute | solution.py:15
  67.6 1.0 pad_maximum_fusion.2
  68.5 0.2 collective-permute-start.6
  68.7 3.7 %collective-permute-start.7 = (f32[8,8,34,1]{2,1,3,0:T(8,128)S(1)}, f32[8,8,34,1]{2,1,3,0:T(8,128)S(1)}, u32[]{:S(2)}, u32[]{:S(2)}) collective-permute-start(f32[8,8,34,1]{2,1,3,0:T(8,128)S(1)} %get-tuple-element.15), channel_id=1, source_target_pairs={{1,0},{2,1},{3,2},{0,3},{5,4},{6,5},{7,6},{4,7},{9,8},{10,9},{11,1... | collective-permute-start | bytes 26120 | tf_op jit(solution)/shard_map/ppermute | solution.py:15
  72.4 0.1 mul.173
  72.5 0.1 mul.174
  72.6 1.7 collective-permute-done.6
  74.3 0.0 collective-permute-done.7
  74.3 5.8 %maximum_select_fusion.1 = f32[8,8,34,130]{2,1,3,0:T(8,128)S(1)} fusion(f32[8,8,34,1]{2,1,3,0:T(8,128)S(1)} %collective-permute-done.7, f32[8,8,1,128]{2,1,3,0:T(8,128)} %copy.92, f32[8,8,32,128]{2,1,3,0:T(8,128)} %copy-done.1, f32[8,8,1,128]{2,1,3,0:T(8,128)} %copy.91, f32[8,8,34,1]{2,1,3,0:T(8,128)S(1)} %collective-permute-done.6, ...), kind=kLoop, calls=%fused_computation.2 | loop fusion | flops 1414400 | bytes 2263074 | tf_op jit(solution)/shard_map/jit(_where)/select_n | solution.py:47
  80.1 0.0 copy-start.3
  80.2 0.0 copy-start.4
  80.2 0.0 copy-start.7
  80.2 2.2 %slice_subtract_fusion.9 = (f32[8,7,32,128]{2,1,3,0:T(8,128)S(1)}, f32[8,7,32,128]{2,1,3,0:T(8,128)S(1)}) fusion(f32[8,8,34,130]{2,1,3,0:T(8,128)S(1)} %maximum_select_fusion.1), kind=kLoop, calls=%fused_computation.35 | loop fusion | flops 458752 | bytes 3670016 | tf_op jit(solution)/shard_map/sub | solution.py:27
  82.5 6.0 %fusion.27 = (f32[8,8,32]{2,1,0:T(8,128)S(1)}, f32[8,8,32,128]{2,1,3,0:T(8,128)}) fusion(f32[8,7,32,128]{2,1,3,0:T(8,128)S(1)} %get-tuple-element.19, f32[8,32,128]{1,0,2:T(8,128)S(1)} %copy-done.7, f32[8,7,32,128]{2,1,3,0:T(8,128)S(1)} %get-tuple-element.18, f32[8,32,128]{1,0,2:T(8,128)S(1)} %copy-done.6, f32[8,8,34,130]{2,1,3,0:T(8,128)S(1)} %maximum_select_fusion.1, ...), kind=kLoop, calls=%fused_computation.65 | loop fusion | flops 4454400 | bytes 8921088 | tf_op jit(solution)/shard_map/reduce_sum | solution.py:76
  88.4 19.5 %psum.14 = f32[8,8,32]{2,1,0:T(8,128)S(1)} all-reduce(f32[8,8,32]{2,1,0:T(8,128)S(1)} %get-tuple-element.12), channel_id=1, replica_groups=mesh['lat'=8,'lon'=4] {'lon'}, use_global_device_ids=true, to_apply=%region_1.2 | all-reduce | flops 2048 | bytes 16384 | tf_op jit(solution)/shard_map/psum | solution.py:76
  108.0 2.6 %multiply_add_fusion = f32[8,8,32,128]{2,1,3,0:T(8,128)S(1)} fusion(f32[8,8,32,128]{2,1,3,0:T(8,128)} %get-tuple-element.13, f32[8,8,32]{2,1,0:T(8,128)S(1)} %broadcast_multiply_fusion, f32[32]{0:T(128)S(1)} %convert_multiply_fusion), kind=kLoop, calls=%fused_computation.32 | loop fusion | flops 786432 | bytes 2105472 | tf_op jit(solution)/shard_map/add | solution.py:79
  110.6 1.9 %copy-done.2 = f32[8,8,32,128]{2,1,3,0:T(8,128)} copy-done((f32[8,8,32,128]{2,1,3,0:T(8,128)}, f32[8,8,32,128]{2,1,3,0:T(8,128)S(1)}, u32[]{:S(2)}) %copy-start.2) | copy-done | bytes 1048600
  112.6 3.7 %copy.96 = f32[8,8,32,128]{3,2,1,0:T(8,128)} copy(f32[8,8,32,128]{2,1,3,0:T(8,128)} %copy-done.2) | data formatting | bytes 2097152
  116.2 0.3 copy.93
  116.5 2.0 %fusion.20 = f32[256,8]{1,0:T(8,128)S(1)} fusion(s32[4096]{0:T(1024)S(1)} %bitcast.39, f32[1,8,32,128]{3,2,1,0:T(8,128)S(1)} %bitcast.35, f32[4096]{0:T(1024)S(1)} %bitcast.40), kind=kOutput, calls=%fused_computation.33 | convolution fusion | flops 101744640 | bytes 172032 | tf_op jit(solution)/shard_map/dot_general | solution.py:85
  118.5 1.7 scatter_custom_fusion
  120.1 49.0 %psum.15 = bf16[2048,8]{1,0:T(8,128)(2,1)S(1)} all-reduce(f32[2048,8]{1,0:T(8,128)S(1)} %scatter_custom_fusion), channel_id=1, replica_groups=mesh['lat'=8,'lon'=4] {'lat','lon'}, use_global_device_ids=true, to_apply=%region_3.4 | all-reduce | flops 16384 | bytes 98304 | tf_op jit(solution)/shard_map/psum | solution.py:94
  169.2 0.3 convolution_bitcast_fusion
  169.5 0.1 copy.95
  169.6 0.0 all-gather.2.cloned.1.call-done
  169.7 2.7 %convolution_add_fusion = f32[64,416]{1,0:T(8,128)} fusion(bf16[64,2048]{1,0:T(8,128)(2,1)S(1)} %copy-done, bf16[2048,416]{1,0:T(8,128)(2,1)} %all-gather.2.cloned.1.call-done, f32[64,416]{1,0:T(8,128)S(1)} %copy.95, f32[416]{0:T(512)S(1)} %mul.174), kind=kOutput, calls=%fused_computation.39 | convolution fusion | flops 109105152 | bytes 2180736 | tf_op jit(solution)/shard_map/dot_general | solution.py:67
  (19 shorter events, 0.1 us)
Async XLA Ops:
  7.2 162.0 %copy-start = (bf16[64,2048]{1,0:T(8,128)(2,1)S(1)}, bf16[64,2048]{1,0:T(8,128)(2,1)}, u32[]{:S(2)}) copy-start(bf16[64,2048]{1,0:T(8,128)(2,1)} %param.17) | copy-start | bytes 786436
  7.2 162.5 %all-gather.2.cloned.1.call-start = ((), (), s32[]{:S(2)}) async-start(), calls=%async_computation | async-start | bytes 2162688 | tf_op jit(solution)/shard_map/all_gather | solution.py:69
  8.3 9.1 %collective-permute-start = (f32[8,8,1,128]{3,1,2,0:T(8,128)S(1)}, f32[8,8,1,128]{3,1,2,0:T(8,128)S(1)}, u32[]{:S(2)}, u32[]{:S(2)}) collective-permute-start(f32[8,8,1,128]{3,1,2,0:T(8,128)S(1)} %bitcast.37), channel_id=1, source_target_pairs={{0,4},{4,8},{8,12},{12,16},{16,20},{20,24},{24,28},{28,0},{1,5},{5... | collective-permute-start | bytes 98312 | tf_op jit(solution)/shard_map/ppermute | solution.py:14
  8.9 11.2 %collective-permute-start.1 = (f32[8,8,1,128]{3,1,2,0:T(8,128)S(1)}, f32[8,8,1,128]{3,1,2,0:T(8,128)S(1)}, u32[]{:S(2)}, u32[]{:S(2)}) collective-permute-start(f32[8,8,1,128]{3,1,2,0:T(8,128)S(1)} %bitcast.36), channel_id=1, source_target_pairs={{4,0},{8,4},{12,8},{16,12},{20,16},{24,20},{28,24},{0,28},{5,1},{9... | collective-permute-start | bytes 98312 | tf_op jit(solution)/shard_map/ppermute | solution.py:15
  23.6 9.7 %collective-permute-start.2 = (f32[8,8,34,1]{2,1,3,0:T(8,128)S(1)}, f32[8,8,34,1]{2,1,3,0:T(8,128)S(1)}, u32[]{:S(2)}, u32[]{:S(2)}) collective-permute-start(f32[8,8,34,1]{2,1,3,0:T(8,128)S(1)} %get-tuple-element.16), channel_id=1, source_target_pairs={{0,1},{1,2},{2,3},{3,0},{4,5},{5,6},{6,7},{7,4},{8,9},{9,10},{10,1... | collective-permute-start | bytes 26120 | tf_op jit(solution)/shard_map/ppermute | solution.py:14
  26.0 7.4 %collective-permute-start.3 = (f32[8,8,34,1]{2,1,3,0:T(8,128)S(1)}, f32[8,8,34,1]{2,1,3,0:T(8,128)S(1)}, u32[]{:S(2)}, u32[]{:S(2)}) collective-permute-start(f32[8,8,34,1]{2,1,3,0:T(8,128)S(1)} %get-tuple-element.17), channel_id=1, source_target_pairs={{1,0},{2,1},{3,2},{0,3},{5,4},{6,5},{7,6},{4,7},{9,8},{10,9},{11,1... | collective-permute-start | bytes 26120 | tf_op jit(solution)/shard_map/ppermute | solution.py:15
  47.6 4.6 %copy-start.1 = (f32[8,8,32,128]{2,1,3,0:T(8,128)}, f32[8,8,32,128]{2,1,3,0:T(8,128)S(1)}, u32[]{:S(2)}) copy-start(f32[8,8,32,128]{2,1,3,0:T(8,128)S(1)} %fusion.13) | copy-start | bytes 3145732
  55.1 7.1 %collective-permute-start.4 = (f32[8,8,1,128]{3,1,2,0:T(8,128)S(1)}, f32[8,8,1,128]{3,1,2,0:T(8,128)S(1)}, u32[]{:S(2)}, u32[]{:S(2)}) collective-permute-start(f32[8,8,1,128]{3,1,2,0:T(8,128)S(1)} %copy.89), channel_id=1, source_target_pairs={{0,4},{4,8},{8,12},{12,16},{16,20},{20,24},{24,28},{28,0},{1,5},{5... | collective-permute-start | bytes 98312 | tf_op jit(solution)/shard_map/ppermute | solution.py:14
  58.0 6.9 %collective-permute-start.5 = (f32[8,8,1,128]{3,1,2,0:T(8,128)S(1)}, f32[8,8,1,128]{3,1,2,0:T(8,128)S(1)}, u32[]{:S(2)}, u32[]{:S(2)}) collective-permute-start(f32[8,8,1,128]{3,1,2,0:T(8,128)S(1)} %copy.90), channel_id=1, source_target_pairs={{4,0},{8,4},{12,8},{16,12},{20,16},{24,20},{28,24},{0,28},{5,1},{9... | collective-permute-start | bytes 98312 | tf_op jit(solution)/shard_map/ppermute | solution.py:15
  68.5 5.8 %collective-permute-start.6 = (f32[8,8,34,1]{2,1,3,0:T(8,128)S(1)}, f32[8,8,34,1]{2,1,3,0:T(8,128)S(1)}, u32[]{:S(2)}, u32[]{:S(2)}) collective-permute-start(f32[8,8,34,1]{2,1,3,0:T(8,128)S(1)} %get-tuple-element.14), channel_id=1, source_target_pairs={{0,1},{1,2},{2,3},{3,0},{4,5},{5,6},{6,7},{7,4},{8,9},{9,10},{10,1... | collective-permute-start | bytes 26120 | tf_op jit(solution)/shard_map/ppermute | solution.py:14
  68.7 5.6 %collective-permute-start.7 = (f32[8,8,34,1]{2,1,3,0:T(8,128)S(1)}, f32[8,8,34,1]{2,1,3,0:T(8,128)S(1)}, u32[]{:S(2)}, u32[]{:S(2)}) collective-permute-start(f32[8,8,34,1]{2,1,3,0:T(8,128)S(1)} %get-tuple-element.15), channel_id=1, source_target_pairs={{1,0},{2,1},{3,2},{0,3},{5,4},{6,5},{7,6},{4,7},{9,8},{10,9},{11,1... | collective-permute-start | bytes 26120 | tf_op jit(solution)/shard_map/ppermute | solution.py:15
  80.1 2.3 %copy-start.3 = (f32[8,32,128]{1,0,2:T(8,128)S(1)}, f32[8,32,128]{1,0,2:T(8,128)}, u32[]{:S(2)}) copy-start(f32[8,32,128]{1,0,2:T(8,128)} %copy.84) | copy-start | bytes 393220
  80.2 2.3 %copy-start.4 = (f32[8,32,128]{1,0,2:T(8,128)S(1)}, f32[8,32,128]{1,0,2:T(8,128)}, u32[]{:S(2)}) copy-start(f32[8,32,128]{1,0,2:T(8,128)} %copy.85) | copy-start | bytes 393220
  80.2 2.3 %copy-start.5 = (f32[8,32,128]{1,0,2:T(8,128)S(1)}, f32[8,32,128]{1,0,2:T(8,128)}, u32[]{:S(2)}) copy-start(f32[8,32,128]{1,0,2:T(8,128)} %copy.86) | copy-start | bytes 393220
  80.2 2.3 %copy-start.6 = (f32[8,32,128]{1,0,2:T(8,128)S(1)}, f32[8,32,128]{1,0,2:T(8,128)}, u32[]{:S(2)}) copy-start(f32[8,32,128]{1,0,2:T(8,128)} %copy.87) | copy-start | bytes 393220
  80.2 2.3 %copy-start.7 = (f32[8,32,128]{1,0,2:T(8,128)S(1)}, f32[8,32,128]{1,0,2:T(8,128)}, u32[]{:S(2)}) copy-start(f32[8,32,128]{1,0,2:T(8,128)} %copy.88) | copy-start | bytes 393220
  110.6 2.0 %copy-start.2 = (f32[8,8,32,128]{2,1,3,0:T(8,128)}, f32[8,8,32,128]{2,1,3,0:T(8,128)S(1)}, u32[]{:S(2)}) copy-start(f32[8,8,32,128]{2,1,3,0:T(8,128)S(1)} %multiply_add_fusion) | copy-start | bytes 3145732
  112.6 3.9 %copy-start.8 = (s32[32,128]{1,0:T(8,128)S(1)}, s32[32,128]{1,0:T(8,128)}, u32[]{:S(2)}) copy-start(s32[32,128]{1,0:T(8,128)} %param.12) | copy-start | bytes 49156
  112.6 3.9 %copy-start.9 = (f32[32,128]{1,0:T(8,128)S(1)}, f32[32,128]{1,0:T(8,128)}, u32[]{:S(2)}) copy-start(f32[32,128]{1,0:T(8,128)} %param.11) | copy-start | bytes 49156
  112.6 3.7 %slice-start = ((f32[8,8,32,128]{2,1,3,0:T(8,128)}), f32[8,1,32,128]{2,1,3,0:T(1,128)S(1)}, s32[]{:S(2)}) async-start(f32[8,8,32,128]{2,1,3,0:T(8,128)} %copy-done.2), calls=%async_computation.1 | async-start | bytes 1048576 | tf_op jit(solution)/shard_map/slice | solution.py:80
Sparse Core Ops, SparseCore 0:
  12.0 58.4 all-gather.1
where the time goes:
time: 180 us; the launch traced here: 179 us
  blocking collectives  68.5 us (38%)
  local copies, waits for them, and re-layouts  38.5 us (21%)
  other arithmetic  35.8 us (20%)
  between operations  15 us (8%)
  starting transfers between devices  14.7 us (8%)
  matrix products  4.95 us (3%)
    psum x1, blocking collectives, shards(): fresh_all = lax.psum(dense, ('lat', 'lon')).astype(jnp.bfloat16)  49 us
    psum x1, blocking collectives, shards(): row_sums = lax.psum(jnp.sum(field, axis=3), 'lon')  19.5 us
    select_n x2, other arithmetic, pole_mask(): return jnp.where(outside[None, None, :, None], 0.0, padded)  11.7 us
    ppermute x4, starting transfers between devices, extended(): after = lax.ppermute(leading, axis, down)  11.6 us
    unnamed x22, local copies, waits for them, and re-layouts  9.28 us
    slice x3, local copies, waits for them, and re-layouts, extended(): last = lax.slice_in_dim(x, length - width, length, axis=dim)  8.58 us
    add x1, other arithmetic, advance(): centre + rates[0] * to_east + rates[1] * to_west + rates[2] * to_north  6.13 us
    reduce_sum x1, other arithmetic, shards(): row_sums = lax.psum(jnp.sum(field, axis=3), 'lon')  5.98 us
  transfers between devices with their start and end apart: 9, of which 1 were waited for; matrix products, arithmetic and copies ran while one was open for 41% of the time, Pallas kernels for 0%

commit v1 on v0

--- a/solution.py
+++ b/solution.py
@@ -91,7 +91,8 @@
     )
     my_regions = lax.dynamic_index_in_dim(tile_regions, my_tile, 0, keepdims=False)
     dense = jnp.zeros((region_count, tracers), jnp.float32).at[my_regions].add(local_sums)
-    fresh_all = lax.psum(dense, ("lat", "lon")).astype(jnp.bfloat16)
+    fit_regions_by_axis = lambda t0, bus_axis: jnp.sum(lax.all_gather(t0, axis_name=bus_axis), 0)
+    fresh_all = fit_regions_by_axis(dense, ("lat", "lon")).astype(jnp.bfloat16)
     added = jnp.dot(covariance, fresh_all, preferred_element_type=jnp.float32)
     week_hot = (jnp.arange(week_cols, dtype=jnp.int32) == week_index[0]).astype(jnp.float32)
     precond = (

time: 180 us -> 372 us (2.07)
  waiting for transfers between devices: 1.77 us -> 239 us
  blocking collectives: 68.5 us -> 15.8 us
  other arithmetic: 35.8 us -> 44.7 us
    all_gather x0 -> x1, waiting for transfers between devices: none -> 187 us  [shards(): lax.all_gather(t0, axis_name=bus_axis)]
    psum x1 -> x0, blocking collectives: 49 us -> none  [shards(): fresh_all = lax.psum(dense, ('lat', 'lon')).astype(jnp.bfloat16)]
    all_gather x1, waiting for transfers between devices: 0.02 us -> 44.9 us  [shards(): lax.all_gather(grad_in, ('lat', 'lon'), axis=0, tiled=True)]
    reduce_sum x0 -> x1, other arithmetic: none -> 12.2 us  [shards(): jnp.sum(lax.all_gather(t0, axis_name=bus_axis), 0)]
    ppermute x4, waiting for transfers between devices: 1.72 us -> 5.99 us  [extended(): before = lax.ppermute(last, axis, up)]
    psum x1, blocking collectives: 19.5 us -> 15.8 us  [shards(): row_sums = lax.psum(jnp.sum(field, axis=3), 'lon')]
    unnamed x22 -> x30, local copies, waits for them, and re-layouts: 9.28 us -> 9.39 us
  transfers between devices with their start and end apart: 9 -> 10, of which waited for: 1 -> 6; matrix products, arithmetic and copies ran while one was open for 41% -> 10% of each run, Pallas kernels for 0% -> 0%
where the time goes in v1:
time: 372 us
  waiting for transfers between devices  239 us (64%)
  other arithmetic  44.7 us (12%)
  local copies, waits for them, and re-layouts  38.8 us (10%)
  blocking collectives  15.8 us (4%)
  between operations  15 us (4%)
  starting transfers between devices  13 us (3%)
  matrix products  4.95 us (1%)
    all_gather x1, waiting for transfers between devices, shards(): lax.all_gather(t0, axis_name=bus_axis)  187 us
    all_gather x1, waiting for transfers between devices, shards(): lax.all_gather(grad_in, ('lat', 'lon'), axis=0, tiled=True)  44.9 us
    psum x1, blocking collectives, shards(): row_sums = lax.psum(jnp.sum(field, axis=3), 'lon')  15.8 us
    ppermute x4, starting transfers between devices, extended(): after = lax.ppermute(leading, axis, down)  12.7 us
    reduce_sum x1, other arithmetic, shards(): jnp.sum(lax.all_gather(t0, axis_name=bus_axis), 0)  12.2 us
    unnamed x30, local copies, waits for them, and re-layouts  9.39 us
    slice x3, local copies, waits for them, and re-layouts, extended(): last = lax.slice_in_dim(x, length - width, length, axis=dim)  8.57 us
    select_n x2, other arithmetic, pole_mask(): return jnp.where(outside[None, None, :, None], 0.0, padded)  8.17 us
  transfers between devices with their start and end apart: 10, of which 6 were waited for; matrix products, arithmetic and copies ran while one was open for 10% of the time, Pallas kernels for 0%

profile of v1, /device:TPU:0, one launch (start us, length us, event | category | flops | bytes accessed | tf_op | source)
XLA Modules:
  0.0 371.6 jit_solution(13629089094419648733)
XLA Ops:
  7.2 0.0 copy-start
  7.2 0.0 all-gather.6.cloned.1.call-start
  7.2 1.1 fusion.30
  8.3 3.4 collective-permute-start.1
  11.8 0.0 collective-permute-start
  11.8 1.3 slice_bitcast_fusion.5
  13.0 3.7 copy.83
  16.7 0.0 collective-permute-done.1
  16.7 2.6 copy.84
  19.3 0.0 collective-permute-done
  19.3 2.7 copy.82
  21.9 0.9 pad_maximum_fusion.5
  22.9 3.7 collective-permute-start.3
  26.5 0.0 collective-permute-start.2
  26.6 0.2 copy.90
  26.8 1.0 copy.89
  27.8 1.0 copy.88
  28.9 1.0 copy.87
  29.8 1.0 copy.86
  30.9 1.0 copy.85
  31.9 0.4 collective-permute-done.2
  32.3 5.8 %maximum_select_fusion = f32[8,8,34,130]{2,1,3,0:T(8,128)S(1)} fusion(f32[8,8,34,1]{2,1,3,0:T(8,128)S(1)} %collective-permute-done.3, f32[8,8,1,128]{2,1,3,0:T(8,128)} %copy.84, f32[8,8,32,128]{2,1,3,0:T(8,128)} %copy.83, f32[8,8,1,128]{2,1,3,0:T(8,128)} %copy.82, f32[8,8,34,1]{2,1,3,0:T(8,128)S(1)} %collective-permute-done.2, pred[34]{0:T(512)(128)(4,1)S(1)} %and_or_fusion), kind=kLoop, calls=%fused_computation.1 | loop fusion | flops 1414400 | bytes 2263074 | tf_op jit(solution)/shard_map/jit(_where)/select_n | solution.py:47
  38.1 2.2 slice_subtract_fusion.11
  40.3 6.1 %fusion.13 = f32[8,8,32,128]{2,1,3,0:T(8,128)S(1)} fusion(f32[8,8,34,130]{2,1,3,0:T(8,128)S(1)} %maximum_select_fusion, f32[8,7,32,128]{2,1,3,0:T(8,128)S(1)} %get-tuple-element.21, f32[8,7,32,128]{2,1,3,0:T(8,128)S(1)} %get-tuple-element.20, f32[8,32,128]{1,0,2:T(8,128)S(1)} %copy.90, f32[8,32,128]{1,0,2:T(8,128)} %copy.89, f32[8,32,128]{1,0,2:T(8,128)} %copy.88, ...), kind=kLoop, calls=%fused_computation.21 | loop fusion | flops 4194304 | bytes 8912896 | tf_op jit(solution)/shard_map/add | solution.py:30
  46.5 4.6 %fusion.29 = (f32[8,8,1,128]{2,1,3,0:T(8,128)}, f32[8,8,1,128]{2,1,3,0:T(8,128)}) fusion(f32[8,8,32,128]{2,1,3,0:T(8,128)S(1)} %fusion.13), kind=kLoop, calls=%fused_computation.66 | loop fusion | bytes 131072 | tf_op jit(solution)/shard_map/slice | solution.py:12
  51.1 2.9 copy.92
  54.0 2.0 collective-permute-start.5
  56.0 2.8 copy.91
  58.8 0.2 collective-permute-start.4
  59.1 0.0 collective-permute-done.5
  59.1 2.7 copy.94
  61.8 1.5 collective-permute-done.4
  63.3 2.7 copy.93
  66.0 1.1 pad_maximum_fusion.2
  67.1 3.6 collective-permute-start.7
  70.7 0.0 collective-permute-start.6
  70.7 0.7 compare_select_fusion
  71.4 0.9 collective-permute-done.7
  72.3 4.1 %collective-permute-done.6 = f32[8,8,34,1]{2,1,3,0:T(8,128)S(1)} collective-permute-done((f32[8,8,34,1]{2,1,3,0:T(8,128)S(1)}, f32[8,8,34,1]{2,1,3,0:T(8,128)S(1)}, u32[]{:S(2)}, u32[]{:S(2)}) %collective-permute-start.6) | collective-permute-done | bytes 8736 | tf_op jit(solution)/shard_map/ppermute | solution.py:14
  76.4 2.3 maximum_select_fusion.1
  78.7 0.0 copy-start.6
  78.8 2.2 slice_subtract_fusion.9
  81.1 6.0 %fusion.27 = (f32[8,8,32]{2,1,0:T(8,128)S(1)}, f32[8,8,32,128]{2,1,3,0:T(8,128)}) fusion(f32[8,7,32,128]{2,1,3,0:T(8,128)S(1)} %get-tuple-element.19, f32[8,32,128]{1,0,2:T(8,128)S(1)} %copy.90, f32[8,7,32,128]{2,1,3,0:T(8,128)S(1)} %get-tuple-element.18, f32[8,32,128]{1,0,2:T(8,128)S(1)} %copy-done.6, f32[8,8,34,130]{2,1,3,0:T(8,128)S(1)} %maximum_select_fusion.1, ...), kind=kLoop, calls=%fused_computation.65 | loop fusion | flops 4454400 | bytes 8921088 | tf_op jit(solution)/shard_map/reduce_sum | solution.py:76
  87.1 15.8 %psum.7 = f32[8,8,32]{2,1,0:T(8,128)S(1)} all-reduce(f32[8,8,32]{2,1,0:T(8,128)S(1)} %get-tuple-element.12), channel_id=1, replica_groups=mesh['lat'=8,'lon'=4] {'lon'}, use_global_device_ids=true, to_apply=%region_1.2 | all-reduce | flops 2048 | bytes 16384 | tf_op jit(solution)/shard_map/psum | solution.py:76
  102.8 0.0 copy-start.11
  102.8 0.0 copy-start.12
  102.9 2.6 multiply_add_fusion
  105.5 2.1 copy-done.5
  107.6 0.3 slice.146
  107.9 0.3 copy.95
  108.2 2.0 fusion.20
  110.1 2.4 scatter_custom_fusion
  112.5 0.0 all-gather.6.cloned.1.call-update
  112.6 0.0 all-gather.4.cloned.1.call-start
  112.6 0.7 all-gather.4.cloned.1.call-update
  114.0 0.1 mul.173
  114.0 0.1 mul.174
  114.1 3.6 copy.98
  117.7 186.8 %all-gather.6.cloned.1.call-done = f32[65536,8]{1,0:T(8,128)} async-done(((f32[2048,8]{1,0:T(8,128)}), f32[65536,8]{1,0:T(8,128)}) %all-gather.6.cloned.1.call-update) | async-done | bytes 2097168 | tf_op jit(solution)/shard_map/all_gather | solution.py:94
  304.5 12.2 %reduce_sum.19 = bf16[2048,8]{1,0:T(8,128)(2,1)S(1)} reduce(f32[32,2048,8]{2,1,0:T(8,128)} %bitcast.36, f32[]{:T(128)} %constant.8.clone.1), dimensions={0}, to_apply=%region_3.4 | reduce | flops 507904 | bytes 2129924 | tf_op jit(solution)/shard_map/reduce_sum | solution.py:94
  316.7 0.3 convolution_bitcast_fusion
  317.0 0.1 copy.97
  317.1 44.9 %all-gather.4.cloned.1.call-done = bf16[2048,416]{1,0:T(8,128)(2,1)} async-done(((bf16[64,416]{1,0:T(8,128)(2,1)}), bf16[2048,416]{1,0:T(8,128)(2,1)}) %all-gather.4.cloned.1.call-update) | async-done | bytes 1703952 | tf_op jit(solution)/shard_map/all_gather | solution.py:69
  362.0 2.7 convolution_add_fusion
  (29 shorter events, 0.1 us)
Async XLA Ops:
  7.2 309.5 %copy-start = (bf16[64,2048]{1,0:T(8,128)(2,1)S(1)}, bf16[64,2048]{1,0:T(8,128)(2,1)}, u32[]{:S(2)}) copy-start(bf16[64,2048]{1,0:T(8,128)(2,1)} %param.17) | copy-start | bytes 786436
  7.2 297.3 %all-gather.6.cloned.1.call-start = ((), (), s32[]{:S(2)}) async-start(), calls=%async_computation.1 | async-start | bytes 34603008 | tf_op jit(solution)/shard_map/all_gather | solution.py:94
  8.3 8.3 %collective-permute-start.1 = (f32[8,8,1,128]{3,1,2,0:T(8,128)S(1)}, f32[8,8,1,128]{3,1,2,0:T(8,128)S(1)}, u32[]{:S(2)}, u32[]{:S(2)}) collective-permute-start(f32[8,8,1,128]{3,1,2,0:T(8,128)S(1)} %bitcast.39), channel_id=1, source_target_pairs={{4,0},{8,4},{12,8},{16,12},{20,16},{24,20},{28,24},{0,28},{5,1},{9... | collective-permute-start | bytes 98312 | tf_op jit(solution)/shard_map/ppermute | solution.py:15
  11.8 7.5 %collective-permute-start = (f32[8,8,1,128]{3,1,2,0:T(8,128)S(1)}, f32[8,8,1,128]{3,1,2,0:T(8,128)S(1)}, u32[]{:S(2)}, u32[]{:S(2)}) collective-permute-start(f32[8,8,1,128]{3,1,2,0:T(8,128)S(1)} %bitcast.38), channel_id=1, source_target_pairs={{0,4},{4,8},{8,12},{12,16},{16,20},{20,24},{24,28},{28,0},{1,5},{5... | collective-permute-start | bytes 98312 | tf_op jit(solution)/shard_map/ppermute | solution.py:14
  22.9 9.0 %collective-permute-start.3 = (f32[8,8,34,1]{2,1,3,0:T(8,128)S(1)}, f32[8,8,34,1]{2,1,3,0:T(8,128)S(1)}, u32[]{:S(2)}, u32[]{:S(2)}) collective-permute-start(f32[8,8,34,1]{2,1,3,0:T(8,128)S(1)} %get-tuple-element.17), channel_id=1, source_target_pairs={{1,0},{2,1},{3,2},{0,3},{5,4},{6,5},{7,6},{4,7},{9,8},{10,9},{11,1... | collective-permute-start | bytes 26120 | tf_op jit(solution)/shard_map/ppermute | solution.py:15
  26.5 5.7 %collective-permute-start.2 = (f32[8,8,34,1]{2,1,3,0:T(8,128)S(1)}, f32[8,8,34,1]{2,1,3,0:T(8,128)S(1)}, u32[]{:S(2)}, u32[]{:S(2)}) collective-permute-start(f32[8,8,34,1]{2,1,3,0:T(8,128)S(1)} %get-tuple-element.16), channel_id=1, source_target_pairs={{0,1},{1,2},{2,3},{3,0},{4,5},{5,6},{6,7},{7,4},{8,9},{9,10},{10,1... | collective-permute-start | bytes 26120 | tf_op jit(solution)/shard_map/ppermute | solution.py:14
  46.5 4.6 %copy-start.1 = (f32[8,8,32,128]{2,1,3,0:T(8,128)}, f32[8,8,32,128]{2,1,3,0:T(8,128)S(1)}, u32[]{:S(2)}) copy-start(f32[8,8,32,128]{2,1,3,0:T(8,128)S(1)} %fusion.13) | copy-start | bytes 3145732
  51.1 8.0 %copy-start.13 = (s32[32]{0:T(128)S(1)}, s32[32]{0:T(128)}, u32[]{:S(2)}) copy-start(s32[32]{0:T(128)} %param.14) | copy-start | bytes 388
  54.0 5.2 %collective-permute-start.5 = (f32[8,8,1,128]{3,1,2,0:T(8,128)S(1)}, f32[8,8,1,128]{3,1,2,0:T(8,128)S(1)}, u32[]{:S(2)}, u32[]{:S(2)}) collective-permute-start(f32[8,8,1,128]{3,1,2,0:T(8,128)S(1)} %copy.92), channel_id=1, source_target_pairs={{4,0},{8,4},{12,8},{16,12},{20,16},{24,20},{28,24},{0,28},{5,1},{9... | collective-permute-start | bytes 98312 | tf_op jit(solution)/shard_map/ppermute | solution.py:15
  58.8 4.5 %collective-permute-start.4 = (f32[8,8,1,128]{3,1,2,0:T(8,128)S(1)}, f32[8,8,1,128]{3,1,2,0:T(8,128)S(1)}, u32[]{:S(2)}, u32[]{:S(2)}) collective-permute-start(f32[8,8,1,128]{3,1,2,0:T(8,128)S(1)} %copy.91), channel_id=1, source_target_pairs={{0,4},{4,8},{8,12},{12,16},{16,20},{20,24},{24,28},{28,0},{1,5},{5... | collective-permute-start | bytes 98312 | tf_op jit(solution)/shard_map/ppermute | solution.py:14
  66.0 10.4 %copy-start.2 = (f32[8,8,32,128]{2,1,3,0:T(8,128)S(1)}, f32[8,8,32,128]{2,1,3,0:T(8,128)}, u32[]{:S(2)}) copy-start(f32[8,8,32,128]{2,1,3,0:T(8,128)} %copy-done.1) | copy-start | bytes 3145732
  66.0 10.4 %copy-start.3 = (f32[8,8,1,128]{2,1,3,0:T(8,128)S(1)}, f32[8,8,1,128]{2,1,3,0:T(8,128)}, u32[]{:S(2)}) copy-start(f32[8,8,1,128]{2,1,3,0:T(8,128)} %copy.94) | copy-start | bytes 98308
  66.0 10.4 %copy-start.4 = (f32[8,8,1,128]{2,1,3,0:T(8,128)S(1)}, f32[8,8,1,128]{2,1,3,0:T(8,128)}, u32[]{:S(2)}) copy-start(f32[8,8,1,128]{2,1,3,0:T(8,128)} %copy.93) | copy-start | bytes 98308
  67.1 5.2 %collective-permute-start.7 = (f32[8,8,34,1]{2,1,3,0:T(8,128)S(1)}, f32[8,8,34,1]{2,1,3,0:T(8,128)S(1)}, u32[]{:S(2)}, u32[]{:S(2)}) collective-permute-start(f32[8,8,34,1]{2,1,3,0:T(8,128)S(1)} %get-tuple-element.15), channel_id=1, source_target_pairs={{1,0},{2,1},{3,2},{0,3},{5,4},{6,5},{7,6},{4,7},{9,8},{10,9},{11,1... | collective-permute-start | bytes 26120 | tf_op jit(solution)/shard_map/ppermute | solution.py:15
  70.7 5.7 %collective-permute-start.6 = (f32[8,8,34,1]{2,1,3,0:T(8,128)S(1)}, f32[8,8,34,1]{2,1,3,0:T(8,128)S(1)}, u32[]{:S(2)}, u32[]{:S(2)}) collective-permute-start(f32[8,8,34,1]{2,1,3,0:T(8,128)S(1)} %get-tuple-element.14), channel_id=1, source_target_pairs={{0,1},{1,2},{2,3},{3,0},{4,5},{5,6},{6,7},{7,4},{8,9},{9,10},{10,1... | collective-permute-start | bytes 26120 | tf_op jit(solution)/shard_map/ppermute | solution.py:14
  78.7 2.3 copy-start.6
  78.7 2.3 copy-start.7
  78.8 2.3 copy-start.8
  78.8 2.3 copy-start.9
  78.8 2.3 copy-start.10
  102.8 5.3 %copy-start.11 = (s32[32,128]{1,0:T(8,128)S(1)}, s32[32,128]{1,0:T(8,128)}, u32[]{:S(2)}) copy-start(s32[32,128]{1,0:T(8,128)} %param.12) | copy-start | bytes 49156
  102.8 5.3 %copy-start.12 = (f32[32,128]{1,0:T(8,128)S(1)}, f32[32,128]{1,0:T(8,128)}, u32[]{:S(2)}) copy-start(f32[32,128]{1,0:T(8,128)} %param.11) | copy-start | bytes 49156
  105.5 2.1 copy-start.5
  112.6 249.4 %all-gather.4.cloned.1.call-start = ((), (), s32[]{:S(2)}) async-start(), calls=%async_computation | async-start | bytes 2162688 | tf_op jit(solution)/shard_map/all_gather | solution.py:69
Sparse Core Ops, SparseCore 0:
  112.7 191.7 all-gather.5
  307.4 54.5 all-gather.3
